TPU v7x, 32 devices: a whole 2x2x4 slice. The times are simulated.
32 devices in a mesh: gx: 4 (over z), gy: 4 (over y, x), gz: 2 (over core).
Axes of the slice: x: 2, y: 2, z: 4, core: 2. Of those that a mesh axis runs over, the one named last changes fastest.
Arguments:
- species_field: float32 [8, 384, 6144], P('gz', 'gx', 'gy'), may hold values from -24 to 24
- start_first: float32 [384, 96], replicated, may hold values from -0.3125 to 0.3125
- start_second: float32 [384, 96], replicated, may hold values from -0.3125 to 0.3125
Outputs:
- factor_first: float32 [384, 96], replicated
- factor_second: float32 [384, 96], replicated
- core_tensor: float32 [16, 8, 96, 96], P('gx', 'gz', 'gy')
All inputs are finite; a program needn't handle non-finite values.
Results may differ from a plain program's by a relative error of at most 0.0003.
Values sent between devices are 32-bit elements; how exact they have to be, the bound alone decides.
A program may use at most 64 MiB of HBM per device.

v0:
```python
import jax
import jax.numpy as jnp
from jax import lax
from jax.sharding import PartitionSpec as P

S = 16
ITERS = 2
exact_precision = lax.Precision.HIGHEST


def leading(image_fn, start):
    current = start
    for turn in range(ITERS):
        images = image_fn(current)
        cross_gram = jnp.dot(images.T, images, precision=exact_precision)
        lower_factor = jnp.linalg.cholesky(cross_gram)
        current = lax.linalg.triangular_solve(
            lower_factor, images, left_side=False, lower=True, transpose_a=True
        )
    return current


def local(species_field, start_first, start_second):
    fibres = lax.all_to_all(species_field, "gx", split_axis=2, concat_axis=1, tiled=True)
    partial_gram = jnp.einsum("zic,zjc->ij", fibres, fibres, precision=exact_precision)
    gram_first = lax.psum(partial_gram, ("gx", "gy", "gz"))

    def image_first(current):
        return jnp.dot(gram_first, current, precision=exact_precision)

    factor_first = leading(image_first, start_first)
    cells = fibres.shape[2] // S
    blocks = fibres.reshape(fibres.shape[0], fibres.shape[1], cells, S)
    projected = jnp.einsum("ziks,ir->zrsk", blocks, factor_first, precision=exact_precision)
    rows_second = lax.all_to_all(
        lax.all_to_all(projected, "gx", split_axis=2, concat_axis=3, tiled=True),
        "gy",
        split_axis=1,
        concat_axis=3,
        tiled=True,
    )
    flat_rows = rows_second.reshape(-1, rows_second.shape[3])
    partial_second = jnp.dot(flat_rows.T, flat_rows, precision=exact_precision)
    gram_second = lax.psum(partial_second, ("gx", "gy", "gz"))

    def image_second(current):
        return jnp.dot(gram_second, current, precision=exact_precision)

    factor_second = leading(image_second, start_second)
    core_local = jnp.einsum("zrsj,jq->szrq", rows_second, factor_second, precision=exact_precision)
    return (factor_first, factor_second, core_local)


def solution(mesh):
    return jax.shard_map(
        local,
        mesh=mesh,
        in_specs=(P("gz", "gx", "gy"), P(), P()),
        out_specs=(P(), P(), P("gx", "gz", "gy", None)),
        check_vma=False,
    )
```

profile of v0, /device:TPU:0, one launch (start us, length us, event | category | flops | bytes accessed | tf_op | source)
XLA Modules:
  0.0 482.7 jit_solution(708190136586059608)
XLA Ops:
  7.2 0.0 copy-start
  7.2 0.0 all-reduce.3.cloned.1.call-start
  7.2 4.5 copy.38
  11.8 77.0 %all_to_all.54 = f32[4,96,1536]{1,0,2:T(4,128)S(1)} all-to-all(f32[4,96,1536]{1,0,2:T(4,128)} %copy.38), channel_id=1, replica_groups=mesh['gx'=4,'gy'=4,'gz'=2] {'gx'}, dimensions={2} | all-to-all | bytes 4718592 | tf_op jit(solution)/shard_map/all_to_all | solution.py:24
  88.8 2.8 copy.40
  91.5 7.1 %convolution_bitcast_fusion = f32[384,384]{1,0:T(8,128)} fusion(f32[4,384,384]{2,1,0:T(8,128)} %bitcast.105), kind=kOutput, calls=%fused_computation.4 | convolution fusion | flops 2717908992 | bytes 2949120 | tf_op jit(solution)/shard_map/zic,zjc->ij/dot_general | solution.py:25
  98.7 0.0 all-reduce.3.cloned.1.call-update
  98.7 0.0 all-reduce.5.cloned.1.call-start
  98.7 3.7 copy.63
  102.4 3.6 reshape.25
  106.0 120.4 %all-reduce.3.cloned.1.call-done = f32[384,384]{1,0:T(8,128)} async-done(((f32[384,384]{1,0:T(8,128)}), f32[384,384]{1,0:T(8,128)}) %all-reduce.3.cloned.1.call-update) | async-done | bytes 589840 | tf_op jit(solution)/shard_map/psum | solution.py:26
  226.4 0.0 copy-done
  226.4 1.9 fusion.23
  228.2 0.3 fusion.24
  228.6 0.1 copy.41
  228.7 8.8 %cholesky.74 = f32[96,96]{1,0:T(8,128)S(1)} custom-call(f32[96,96]{1,0:T(8,128)S(1)} %fusion.20), custom_call_target="Cholesky" | custom-call | tf_op jit(solution)/shard_map/jit(cholesky)/cholesky | solution.py:16
  237.5 0.6 compare_reduce_fusion.3
  238.1 0.7 fusion.7
  238.8 7.4 %custom-call.8 = f32[1,96,96]{1,2,0:T(8,128)S(1)} custom-call(f32[1,96,96]{2,1,0:T(8,128)S(1)} %fusion.7), custom_call_target="InvertDiagBlocksLowerTriangular" | custom-call | tf_op jit(solution)/shard_map/triangular_solve/custom-call.0 | solution.py:17
  246.2 0.3 convolution_bitcast_fusion.3
  246.5 0.7 fusion.25
  247.2 0.3 fusion.26
  247.6 0.1 copy.42
  247.7 8.8 %cholesky.85 = f32[96,96]{1,0:T(8,128)S(1)} custom-call(f32[96,96]{1,0:T(8,128)S(1)} %fusion.18), custom_call_target="Cholesky" | custom-call | tf_op jit(solution)/shard_map/jit(cholesky)/cholesky | solution.py:16
  256.5 0.6 compare_reduce_fusion.2
  257.2 0.7 fusion.8
  257.8 7.4 %custom-call.9 = f32[1,96,96]{1,2,0:T(8,128)S(1)} custom-call(f32[1,96,96]{2,1,0:T(8,128)S(1)} %fusion.8), custom_call_target="InvertDiagBlocksLowerTriangular" | custom-call | tf_op jit(solution)/shard_map/triangular_solve/custom-call.0 | solution.py:17
  265.2 0.3 fusion.16
  265.5 0.0 copy-start.3
  265.5 2.6 fusion.2
  268.2 0.1 copy.44
  268.3 23.2 %all_to_all.55 = f32[4,96,16,24]{1,3,0,2:T(8,128)S(1)} all-to-all(f32[4,96,16,24]{1,3,0,2:T(8,128)S(1)} %copy.44), channel_id=1, replica_groups=mesh['gx'=4,'gy'=4,'gz'=2] {'gx'}, dimensions={2} | all-to-all | bytes 1179648 | tf_op jit(solution)/shard_map/all_to_all | solution.py:36
  291.5 0.1 copy.46
  291.6 0.5 copy.47
  292.1 13.3 %all_to_all.56 = f32[4,96,4,96]{3,2,0,1:T(4,128)S(1)} all-to-all(f32[4,96,4,96]{3,2,0,1:T(4,128)S(1)} %copy.47), channel_id=1, replica_groups=mesh['gx'=4,'gy'=4,'gz'=2] {'gy'}, dimensions={1} | all-to-all | bytes 1179648 | tf_op jit(solution)/shard_map/all_to_all | solution.py:35
  305.4 0.3 copy.48
  305.6 0.2 copy.49
  305.8 0.4 reshape.26
  306.2 0.0 copy-start.5
  306.3 2.1 fusion.27
  308.4 0.0 all-reduce.5.cloned.1.call-update
  308.4 0.2 copy.52
  308.6 0.4 all_to_all.50
  309.0 126.3 %all-reduce.5.cloned.1.call-done = f32[384,384]{1,0:T(8,128)} async-done(((f32[384,384]{1,0:T(8,128)}), f32[384,384]{1,0:T(8,128)}) %all-reduce.5.cloned.1.call-update) | async-done | bytes 589840 | tf_op jit(solution)/shard_map/psum | solution.py:44
  435.3 1.9 fusion.28
  437.2 0.3 fusion.29
  437.5 0.1 copy.50
  437.6 8.8 %cholesky.96 = f32[96,96]{1,0:T(8,128)S(1)} custom-call(f32[96,96]{1,0:T(8,128)S(1)} %fusion.15), custom_call_target="Cholesky" | custom-call | tf_op jit(solution)/shard_map/jit(cholesky)/cholesky | solution.py:16
  446.4 0.6 compare_reduce_fusion.1
  447.1 0.7 fusion.9
  447.7 7.4 %custom-call.10 = f32[1,96,96]{1,2,0:T(8,128)S(1)} custom-call(f32[1,96,96]{2,1,0:T(8,128)S(1)} %fusion.9), custom_call_target="InvertDiagBlocksLowerTriangular" | custom-call | tf_op jit(solution)/shard_map/triangular_solve/custom-call.0 | solution.py:17
  455.1 0.3 convolution_bitcast_fusion.2
  455.5 0.7 fusion.30
  456.2 0.3 fusion.31
  456.5 0.1 copy.51
  456.6 8.8 %cholesky.107 = f32[96,96]{1,0:T(8,128)S(1)} custom-call(f32[96,96]{1,0:T(8,128)S(1)} %fusion.13), custom_call_target="Cholesky" | custom-call | tf_op jit(solution)/shard_map/jit(cholesky)/cholesky | solution.py:16
  465.5 0.6 compare_reduce_fusion
  466.1 0.7 fusion.10
  466.8 7.4 %custom-call.11 = f32[1,96,96]{1,2,0:T(8,128)S(1)} custom-call(f32[1,96,96]{2,1,0:T(8,128)S(1)} %fusion.10), custom_call_target="InvertDiagBlocksLowerTriangular" | custom-call | tf_op jit(solution)/shard_map/triangular_solve/custom-call.0 | solution.py:17
  474.1 0.3 fusion.11
  474.5 0.0 copy-start.4
  474.5 0.6 convolution_bitcast_fusion.1
  475.1 0.7 copy.53
  475.8 0.0 copy-done.4
  (14 shorter events, 0.2 us)
Async XLA Ops:
  7.2 219.2 %copy-start = (f32[384,96]{0,1:T(8,128)S(1)}, f32[384,96]{0,1:T(8,128)}, u32[]{:S(2)}) copy-start(f32[384,96]{0,1:T(8,128)} %param.7) | copy-start | bytes 442372
  7.2 219.2 %all-reduce.3.cloned.1.call-start = ((), (), s32[]{:S(2)}) async-start(), calls=%async_computation.3 | async-start | bytes 1179648 | tf_op jit(solution)/shard_map/psum | solution.py:26
  98.7 336.6 %all-reduce.5.cloned.1.call-start = ((), (), s32[]{:S(2)}) async-start(), calls=%async_computation.4 | async-start | bytes 1179648 | tf_op jit(solution)/shard_map/psum | solution.py:44
  226.4 20.1 %copy-start.1 = (f32[384,384]{1,0:T(8,128)S(1)}, f32[384,384]{1,0:T(8,128)}, u32[]{:S(2)}) copy-start(f32[384,384]{1,0:T(8,128)} %all-reduce.3.cloned.1.call-done) | copy-start | bytes 1769476
  265.5 2.8 copy-start.3
  306.2 129.1 %copy-start.5 = (f32[384,96]{0,1:T(8,128)S(1)}, f32[384,96]{0,1:T(8,128)}, u32[]{:S(2)}) copy-start(f32[384,96]{0,1:T(8,128)} %param.8) | copy-start | bytes 442372
  435.3 20.1 %copy-start.2 = (f32[384,384]{1,0:T(8,128)S(1)}, f32[384,384]{1,0:T(8,128)}, u32[]{:S(2)}) copy-start(f32[384,384]{1,0:T(8,128)} %all-reduce.5.cloned.1.call-done) | copy-start | bytes 1769476
  474.5 1.3 copy-start.4
Sparse Core Ops, SparseCore 0:
  98.8 127.5 all-reduce.2
  308.5 126.7 all-reduce.4
where the time goes:
time: 483 us
  waiting for transfers between devices  247 us (51%)
  blocking collectives  114 us (24%)
  other arithmetic  69.9 us (14%)
  matrix products  20.4 us (4%)
  local copies, waits for them, and re-layouts  17.7 us (4%)
  between operations  14.4 us (3%)
    psum x1, waiting for transfers between devices, local(): gram_second = lax.psum(partial_second, ('gx', 'gy', 'gz'))  126 us
    psum x1, waiting for transfers between devices, local(): gram_first = lax.psum(partial_gram, ('gx', 'gy', 'gz'))  120 us
    all_to_all x1, blocking collectives, local(): lax.all_to_all(species_field, 'gx', split_axis=2, concat_axis=1, tiled=True)  77 us
    another operation x12, other arithmetic, leading(): lower_factor = jnp.linalg.cholesky(cross_gram)  37.8 us
    another operation x8, other arithmetic, leading(): lax.linalg.triangular_solve(lower_factor, images, left_side=False, lower=...  32 us
    all_to_all x1, blocking collectives, local(): lax.all_to_all(projected, 'gx', split_axis=2, concat_axis=3, tiled=True)  23.2 us
    all_to_all x1, blocking collectives, local(): lax.all_to_all(lax.all_to_all(projected, 'gx', split_axis=2, concat_axis=...  13.3 us
  transfers between devices with their start and end apart: 2, of which 2 were waited for; matrix products, arithmetic and copies ran while one was open for 2% of the time, Pallas kernels for 0%

commit v1 on v0

--- a/solution.py
+++ b/solution.py
@@ -21,7 +21,12 @@
 
 
 def local(species_field, start_first, start_second):
-    fibres = lax.all_to_all(species_field, "gx", split_axis=2, concat_axis=1, tiled=True)
+    fibres = jnp.concatenate(
+        lax.all_to_all(
+            jnp.stack(jnp.split(species_field, lax.axis_size("gx"), axis=2)), "gx", 0, 0
+        ),
+        axis=1,
+    )
     partial_gram = jnp.einsum("zic,zjc->ij", fibres, fibres, precision=exact_precision)
     gram_first = lax.psum(partial_gram, ("gx", "gy", "gz"))
 

time: 483 us -> 458 us (0.948)
  blocking collectives: 114 us -> 96.5 us
  local copies, waits for them, and re-layouts: 17.7 us -> 11.4 us
    all_to_all x1, blocking collectives: 77 us -> 60 us  [local(): lax.all_to_all(jnp.stack(jnp.split(species_field, lax.axis_size('gx'), ax...]
    all_to_all x2 -> x0, local copies, waits for them, and re-layouts: 6.45 us -> none  [local(): lax.all_to_all(species_field, 'gx', split_axis=2, concat_axis=1, tiled=True)]
    another operation x0 -> x2, local copies, waits for them, and re-layouts: none -> 5.34 us  [the longest x1 3.54 us: local(): blocks = fibres.reshape(fibres.shape[0], fibres.shape[1], cells, S)]
  transfers between devices with their start and end apart: 2 -> 2, of which waited for: 2 -> 2; matrix products, arithmetic and copies ran while one was open for 2% -> 1% of each run, Pallas kernels for 0% -> 0%
where the time goes in v1:
time: 458 us
  waiting for transfers between devices  248 us (54%)
  blocking collectives  96.5 us (21%)
  other arithmetic  70.1 us (15%)
  matrix products  18.1 us (4%)
  between operations  14.4 us (3%)
  local copies, waits for them, and re-layouts  11.4 us (2%)
    psum x1, waiting for transfers between devices, local(): gram_second = lax.psum(partial_second, ('gx', 'gy', 'gz'))  126 us
    psum x1, waiting for transfers between devices, local(): gram_first = lax.psum(partial_gram, ('gx', 'gy', 'gz'))  121 us
    all_to_all x1, blocking collectives, local(): lax.all_to_all(jnp.stack(jnp.split(species_field, lax.axis_size('gx'), ax...  60 us
    another operation x12, other arithmetic, leading(): lower_factor = jnp.linalg.cholesky(cross_gram)  37.8 us
    another operation x8, other arithmetic, leading(): lax.linalg.triangular_solve(lower_factor, images, left_side=False, lower=...  32 us
    all_to_all x1, blocking collectives, local(): lax.all_to_all(projected, 'gx', split_axis=2, concat_axis=3, tiled=True)  23.2 us
    all_to_all x1, blocking collectives, local(): lax.all_to_all(lax.all_to_all(projected, 'gx', split_axis=2, concat_axis=...  13.3 us
  transfers between devices with their start and end apart: 2, of which 2 were waited for; matrix products, arithmetic and copies ran while one was open for 1% of the time, Pallas kernels for 0%

profile of v1, /device:TPU:0, one launch (start us, length us, event | category | flops | bytes accessed | tf_op | source)
XLA Modules:
  0.0 458.0 jit_solution(16885157511403022289)
XLA Ops:
  7.2 0.0 copy-start
  7.2 0.0 all-reduce.3.cloned.1.call-start
  7.2 1.8 slice_bitcast_fusion.3
  9.0 0.2 pad_maximum_fusion
  9.2 60.0 %all_to_all.41 = f32[4,4,96,384]{3,2,1,0:T(8,128)S(1)} all-to-all(f32[4,4,96,384]{3,2,1,0:T(8,128)S(1)} %pad_maximum_fusion), channel_id=1, replica_groups=mesh['gx'=4,'gy'=4,'gz'=2] {'gx'}, dimensions={0} | all-to-all | bytes 4718592 | tf_op jit(solution)/shard_map/all_to_all | solution.py:25
  69.2 0.2 copy.37
  69.3 4.8 %convolution_bitcast_fusion = f32[384,384]{1,0:T(8,128)} fusion(f32[4,384,384]{2,1,0:T(8,128)S(1)} %bitcast.108), kind=kOutput, calls=%fused_computation.4 | convolution fusion | flops 2717908992 | bytes 2949120 | tf_op jit(solution)/shard_map/zic,zjc->ij/dot_general | solution.py:30
  74.1 0.0 all-reduce.3.cloned.1.call-update
  74.1 0.0 all-reduce.5.cloned.1.call-start
  74.2 2.8 copy.40
  77.0 3.5 reshape_reshape.3
  80.5 121.2 %all-reduce.3.cloned.1.call-done = f32[384,384]{1,0:T(8,128)} async-done(((f32[384,384]{1,0:T(8,128)}), f32[384,384]{1,0:T(8,128)}) %all-reduce.3.cloned.1.call-update) | async-done | bytes 589840 | tf_op jit(solution)/shard_map/psum | solution.py:31
  201.7 1.9 fusion.23
  203.6 0.3 fusion.24
  203.9 0.1 copy.38
  204.1 8.8 %cholesky.74 = f32[96,96]{1,0:T(8,128)S(1)} custom-call(f32[96,96]{1,0:T(8,128)S(1)} %fusion.20), custom_call_target="Cholesky" | custom-call | tf_op jit(solution)/shard_map/jit(cholesky)/cholesky | solution.py:16
  212.9 0.6 compare_reduce_fusion.3
  213.5 0.7 fusion.7
  214.2 7.4 %custom-call.8 = f32[1,96,96]{1,2,0:T(8,128)S(1)} custom-call(f32[1,96,96]{2,1,0:T(8,128)S(1)} %fusion.7), custom_call_target="InvertDiagBlocksLowerTriangular" | custom-call | tf_op jit(solution)/shard_map/triangular_solve/custom-call.0 | solution.py:17
  221.5 0.3 convolution_bitcast_fusion.3
  221.9 0.0 copy-done.1
  221.9 0.7 fusion.25
  222.6 0.3 fusion.26
  223.0 0.1 copy.39
  223.1 8.8 %cholesky.85 = f32[96,96]{1,0:T(8,128)S(1)} custom-call(f32[96,96]{1,0:T(8,128)S(1)} %fusion.18), custom_call_target="Cholesky" | custom-call | tf_op jit(solution)/shard_map/jit(cholesky)/cholesky | solution.py:16
  231.9 0.6 compare_reduce_fusion.2
  232.5 0.7 fusion.8
  233.2 7.4 %custom-call.9 = f32[1,96,96]{1,2,0:T(8,128)S(1)} custom-call(f32[1,96,96]{2,1,0:T(8,128)S(1)} %fusion.8), custom_call_target="InvertDiagBlocksLowerTriangular" | custom-call | tf_op jit(solution)/shard_map/triangular_solve/custom-call.0 | solution.py:17
  240.5 0.3 fusion.16
  240.9 0.0 copy-start.3
  240.9 2.6 fusion.2
  243.6 0.1 copy.42
  243.7 23.2 %all_to_all.42 = f32[4,96,16,24]{1,3,0,2:T(8,128)S(1)} all-to-all(f32[4,96,16,24]{1,3,0,2:T(8,128)S(1)} %copy.42), channel_id=1, replica_groups=mesh['gx'=4,'gy'=4,'gz'=2] {'gx'}, dimensions={2} | all-to-all | bytes 1179648 | tf_op jit(solution)/shard_map/all_to_all | solution.py:41
  266.8 0.1 copy.44
  266.9 0.5 copy.45
  267.4 13.3 %all_to_all.43 = f32[4,96,4,96]{3,2,0,1:T(4,128)S(1)} all-to-all(f32[4,96,4,96]{3,2,0,1:T(4,128)S(1)} %copy.45), channel_id=1, replica_groups=mesh['gx'=4,'gy'=4,'gz'=2] {'gy'}, dimensions={1} | all-to-all | bytes 1179648 | tf_op jit(solution)/shard_map/all_to_all | solution.py:40
  280.8 0.3 copy.46
  281.0 0.2 copy.47
  281.2 0.4 reshape.29
  281.6 0.0 copy-start.5
  281.6 2.1 fusion.27
  283.8 0.0 all-reduce.5.cloned.1.call-update
  283.8 0.2 copy.50
  284.0 0.4 all_to_all.37
  284.4 126.3 %all-reduce.5.cloned.1.call-done = f32[384,384]{1,0:T(8,128)} async-done(((f32[384,384]{1,0:T(8,128)}), f32[384,384]{1,0:T(8,128)}) %all-reduce.5.cloned.1.call-update) | async-done | bytes 589840 | tf_op jit(solution)/shard_map/psum | solution.py:49
  410.7 1.9 fusion.28
  412.5 0.3 fusion.29
  412.9 0.1 copy.48
  413.0 8.8 %cholesky.96 = f32[96,96]{1,0:T(8,128)S(1)} custom-call(f32[96,96]{1,0:T(8,128)S(1)} %fusion.15), custom_call_target="Cholesky" | custom-call | tf_op jit(solution)/shard_map/jit(cholesky)/cholesky | solution.py:16
  421.8 0.6 compare_reduce_fusion.1
  422.4 0.7 fusion.9
  423.1 7.4 %custom-call.10 = f32[1,96,96]{1,2,0:T(8,128)S(1)} custom-call(f32[1,96,96]{2,1,0:T(8,128)S(1)} %fusion.9), custom_call_target="InvertDiagBlocksLowerTriangular" | custom-call | tf_op jit(solution)/shard_map/triangular_solve/custom-call.0 | solution.py:17
  430.5 0.3 convolution_bitcast_fusion.2
  430.8 0.7 fusion.30
  431.5 0.3 fusion.31
  431.9 0.1 copy.49
  432.0 8.8 %cholesky.107 = f32[96,96]{1,0:T(8,128)S(1)} custom-call(f32[96,96]{1,0:T(8,128)S(1)} %fusion.13), custom_call_target="Cholesky" | custom-call | tf_op jit(solution)/shard_map/jit(cholesky)/cholesky | solution.py:16
  440.8 0.6 compare_reduce_fusion
  441.4 0.7 fusion.10
  442.1 7.4 %custom-call.11 = f32[1,96,96]{1,2,0:T(8,128)S(1)} custom-call(f32[1,96,96]{2,1,0:T(8,128)S(1)} %fusion.10), custom_call_target="InvertDiagBlocksLowerTriangular" | custom-call | tf_op jit(solution)/shard_map/triangular_solve/custom-call.0 | solution.py:17
  449.5 0.3 fusion.11
  449.8 0.0 copy-start.4
  449.8 0.6 convolution_bitcast_fusion.1
  450.5 0.7 copy.51
  (15 shorter events, 0.2 us)
Async XLA Ops:
  7.2 194.6 %copy-start = (f32[384,96]{0,1:T(8,128)S(1)}, f32[384,96]{0,1:T(8,128)}, u32[]{:S(2)}) copy-start(f32[384,96]{0,1:T(8,128)} %param.7) | copy-start | bytes 442372
  7.2 194.6 %all-reduce.3.cloned.1.call-start = ((), (), s32[]{:S(2)}) async-start(), calls=%async_computation.3 | async-start | bytes 1179648 | tf_op jit(solution)/shard_map/psum | solution.py:31
  74.1 336.5 %all-reduce.5.cloned.1.call-start = ((), (), s32[]{:S(2)}) async-start(), calls=%async_computation.4 | async-start | bytes 1179648 | tf_op jit(solution)/shard_map/psum | solution.py:49
  201.7 20.1 %copy-start.1 = (f32[384,384]{1,0:T(8,128)S(1)}, f32[384,384]{1,0:T(8,128)}, u32[]{:S(2)}) copy-start(f32[384,384]{1,0:T(8,128)} %all-reduce.3.cloned.1.call-done) | copy-start | bytes 1769476
  240.9 2.8 copy-start.3
  281.6 129.0 %copy-start.5 = (f32[384,96]{0,1:T(8,128)S(1)}, f32[384,96]{0,1:T(8,128)}, u32[]{:S(2)}) copy-start(f32[384,96]{0,1:T(8,128)} %param.8) | copy-start | bytes 442372
  410.7 20.1 %copy-start.2 = (f32[384,384]{1,0:T(8,128)S(1)}, f32[384,384]{1,0:T(8,128)}, u32[]{:S(2)}) copy-start(f32[384,384]{1,0:T(8,128)} %all-reduce.5.cloned.1.call-done) | copy-start | bytes 1769476
  449.8 1.3 copy-start.4
Sparse Core Ops, SparseCore 0:
  74.3 127.4 all-reduce.2
  283.9 126.7 all-reduce.4
